TPU v7x, 32 devices: a whole 2x2x4 slice. The times are simulated.
32 devices in a mesh: grid: 8 (over z, core), vec: 4 (over y, x).
Axes of the slice: x: 2, y: 2, z: 4, core: 2. Of those that a mesh axis runs over, the one named last changes fastest.
Arguments:
- orbitals: bfloat16 [884736, 512], P(('grid', 'vec')), may hold values from -1.296875 to 1.296875
- inverse_panel: bfloat16 [2048, 32], replicated, may hold values from -0.125 to 0.125
- points: int32 [2048], replicated, may hold values from 0 to 884735, as said below
Outputs:
- projected: float32 [2048, 32], P(('grid', 'vec'))
Inputs may be any that keep to these rules, and one draw needn't show every extreme that they name: `points`: distinct cell indices.
All inputs are finite; a program needn't handle non-finite values.
Results may differ from a plain program's by a relative error of at most 0.005.
Values may be sent and summed in bfloat16 or wider, within the bound.
A program may use at most 256 MiB of HBM per device.

v0:
```python
import math
import jax
import jax.numpy as jnp
from jax import lax
from jax.sharding import PartitionSpec as P

NG = 96
SCREEN = 2.25


def wave_tables(count):
    index = lax.iota(jnp.int32, count)
    phase = index[:, None] * index[None, :] % count
    angle = phase.astype(jnp.float32) * (2.0 * math.pi / count)
    return (jnp.cos(angle).astype(jnp.bfloat16), jnp.sin(angle).astype(jnp.bfloat16))


def wavenumber(index, count):
    return jnp.where(index < count // 2, index, index - count).astype(jnp.float32)


def screened(wave_x, wave_y, wave_z):
    squared = (
        wave_x[:, None, None] * wave_x[:, None, None]
        + wave_y[None, :, None] * wave_y[None, :, None]
        + wave_z[None, None, :] * wave_z[None, None, :]
    )
    factor = NG / (2.0 * math.pi) * (NG / (2.0 * math.pi))
    return jnp.where(squared > 0.5, factor / (squared + SCREEN), jnp.float32(0.0))


def mult(data, table, form):
    return jnp.einsum(form, data, table, preferred_element_type=jnp.float32)


def shards(orbitals, inverse_panel, points):
    bf = jnp.bfloat16
    row_count = orbitals.shape[0]
    grid_count = lax.axis_size("grid")
    vec_count = lax.axis_size("vec")
    npoints = points.shape[0]
    offset = (lax.axis_index("grid") * vec_count + lax.axis_index("vec")) * row_count
    local_pos = points - offset
    inside = (local_pos >= 0) & (local_pos < row_count)
    picked = jnp.take(orbitals, jnp.clip(local_pos, 0, row_count - 1), axis=0)
    picked = jnp.where(inside[:, None], picked, jnp.zeros_like(picked)).astype(jnp.float32)
    summed_rows = lax.psum(picked, ("grid", "vec"))
    point_rows = summed_rows.astype(bf)

    def pair_block(block):
        correlation = lax.dot_general(
            block, point_rows, (((1,), (1,)), ((), ())), preferred_element_type=jnp.float32
        )
        return (correlation * correlation).astype(bf)

    pair = lax.map(pair_block, orbitals.reshape(4, row_count // 4, orbitals.shape[1])).reshape(
        row_count, npoints
    )
    fit_cols = lax.dot_general(
        inverse_panel, pair, (((0,), (1,)), ((), ())), preferred_element_type=jnp.float32
    ).astype(bf)
    slab = lax.all_to_all(fit_cols, "vec", split_axis=0, concat_axis=1, tiled=True)
    col_local = slab.shape[0]
    planes = NG // grid_count
    field = slab.reshape(col_local, planes, NG, NG)
    cos_tab, sin_tab = wave_tables(NG)
    z_re = mult(field, cos_tab, "vxyz,zk->vxyk").astype(bf)
    z_im = (-mult(field, sin_tab, "vxyz,zk->vxyk")).astype(bf)
    y_re = (mult(z_re, cos_tab, "vxyz,yk->vxkz") + mult(z_im, sin_tab, "vxyz,yk->vxkz")).astype(bf)
    y_im = (mult(z_im, cos_tab, "vxyz,yk->vxkz") - mult(z_re, sin_tab, "vxyz,yk->vxkz")).astype(bf)
    stacked = jnp.stack([y_re, y_im])
    waves = wavenumber(lax.iota(jnp.int32, NG), NG)
    y_waves = wavenumber(lax.axis_index("grid") * planes + lax.iota(jnp.int32, planes), NG)
    kernel = screened(waves, y_waves, waves)[None]
    piece = lax.all_to_all(stacked, "grid", split_axis=3, concat_axis=2, tiled=True)
    p_re = piece[0]
    p_im = piece[1]
    x_re = mult(p_re, cos_tab, "vxyz,xk->vkyz") + mult(p_im, sin_tab, "vxyz,xk->vkyz")
    x_im = mult(p_im, cos_tab, "vxyz,xk->vkyz") - mult(p_re, sin_tab, "vxyz,xk->vkyz")
    q_re = (x_re * kernel).astype(bf)
    q_im = (x_im * kernel).astype(bf)
    i_re = (mult(q_re, cos_tab, "vxyz,xk->vkyz") - mult(q_im, sin_tab, "vxyz,xk->vkyz")).astype(bf)
    i_im = (mult(q_im, cos_tab, "vxyz,xk->vkyz") + mult(q_re, sin_tab, "vxyz,xk->vkyz")).astype(bf)
    spectrum = lax.all_to_all(
        jnp.stack([i_re, i_im]), "grid", split_axis=2, concat_axis=3, tiled=True
    )
    s_re = spectrum[0]
    s_im = spectrum[1]
    h_re = (mult(s_re, cos_tab, "vxyz,yk->vxkz") - mult(s_im, sin_tab, "vxyz,yk->vxkz")).astype(bf)
    h_im = (mult(s_im, cos_tab, "vxyz,yk->vxkz") + mult(s_re, sin_tab, "vxyz,yk->vxkz")).astype(bf)
    final = mult(h_re, cos_tab, "vxyz,zk->vxyk") - mult(h_im, sin_tab, "vxyz,zk->vxyk")
    potential = (final / float(NG**3)).astype(bf).reshape(col_local, planes * NG * NG)
    pot_rows = lax.all_to_all(potential, "vec", split_axis=1, concat_axis=0, tiled=True)
    scale = 1.0 / math.sqrt(float(NG**3))
    term = lax.dot_general(
        pair, pot_rows, (((0,), (1,)), ((), ())), preferred_element_type=jnp.float32
    )
    partial_block = lax.psum_scatter(
        term * jnp.float32(scale), "grid", scatter_dimension=0, tiled=True
    )
    projected = lax.psum_scatter(partial_block, "vec", scatter_dimension=0, tiled=True)
    return projected


def solution(mesh):
    in_specs = (P(("grid", "vec"), None), P(), P())
    out_specs = P(("grid", "vec"), None)
    return jax.shard_map(shards, mesh=mesh, in_specs=in_specs, out_specs=out_specs, check_vma=False)
```

profile of v0, /device:TPU:0, one launch (start us, length us, event | category | flops | bytes accessed | tf_op | source)
XLA Modules:
  0.0 691.5 jit_solution(2763133241385044677)
XLA Ops:
  8.0 20.3 %gather_fusion = bf16[2048,512]{1,0:T(8,128)(2,1)S(1)} fusion(bf16[27648,512]{1,0:T(8,128)(2,1)} %param.5, s32[2048]{0:T(1024)S(1)} %fusion.73), kind=kCustom, calls=%fused_computation | custom fusion | bytes 4202496 | tf_op jit(solution)/shard_map/jit(_take)/gather | solution.py:45
  28.3 3.4 select_convert_fusion
  31.7 94.7 %all-reduce.1 = bf16[2048,512]{1,0:T(8,128)(2,1)S(1)} all-reduce(f32[2048,512]{1,0:T(8,128)} %select_convert_fusion), channel_id=1, replica_groups=mesh['grid'=8,'vec'=4] {'grid','vec'}, use_global_device_ids=true, to_apply=%region_0.1 | all-reduce | flops 1048576 | bytes 6291456 | tf_op jit(solution)/shard_map/psum | solution.py:47
  126.4 86.1 %while.10 = (s32[]{:T(128)}, bf16[4,6912,2048]{2,1,0:T(8,128)(2,1)}, bf16[4,6912,512]{2,1,0:T(8,128)(2,1)}, bf16[2048,512]{1,0:T(8,128)(2,1)S(1)}, s32[]{:T(128)}) while((s32[]{:T(128)}, bf16[4,6912,2048]{2,1,0:T(8,128)(2,1)}, bf16[4,6912,512]{2,1,0:T(8,128)(2,1)}, bf16[2048,512]{1,0:T(8,128)(2,1)S(1)}, s32[]{:T(128)}) %tuple.28), condition=%wide.region_2.3_spmd, body=%wide.region_1.2_spmd.sunk | while | flops 14523826176 | bytes 37487676 | solution.py:56
  126.4 21.5 %bitcast_dynamic-update-slice_fusion.2 = bf16[4,6912,2048]{2,1,0:T(8,128)(2,1)} fusion(bf16[4,6912,2048]{2,1,0:T(8,128)(2,1)} %get-tuple-element.73, s32[]{:T(128)} %get-tuple-element.72, bf16[2048,512]{1,0:T(8,128)(2,1)S(1)} %get-tuple-element.80, bf16[4,6912,512]{2,1,0:T(8,128)(2,1)} %get-tuple-element.79), kind=kOutput, calls=%fused_computation.2.clone.1 | convolution fusion | flops 14523826176 | bytes 37487616 | tf_op jit(solution)/shard_map/while/body/eval_jaxpr/dot_general | solution.py:51
  147.9 21.5 %bitcast_dynamic-update-slice_fusion.2 = bf16[4,6912,2048]{2,1,0:T(8,128)(2,1)} fusion(bf16[4,6912,2048]{2,1,0:T(8,128)(2,1)} %get-tuple-element.73, s32[]{:T(128)} %get-tuple-element.72, bf16[2048,512]{1,0:T(8,128)(2,1)S(1)} %get-tuple-element.80, bf16[4,6912,512]{2,1,0:T(8,128)(2,1)} %get-tuple-element.79), kind=kOutput, calls=%fused_computation.2.clone.1 | convolution fusion | flops 14523826176 | bytes 37487616 | tf_op jit(solution)/shard_map/while/body/eval_jaxpr/dot_general | solution.py:51
  169.4 21.5 %bitcast_dynamic-update-slice_fusion.2 = bf16[4,6912,2048]{2,1,0:T(8,128)(2,1)} fusion(bf16[4,6912,2048]{2,1,0:T(8,128)(2,1)} %get-tuple-element.73, s32[]{:T(128)} %get-tuple-element.72, bf16[2048,512]{1,0:T(8,128)(2,1)S(1)} %get-tuple-element.80, bf16[4,6912,512]{2,1,0:T(8,128)(2,1)} %get-tuple-element.79), kind=kOutput, calls=%fused_computation.2.clone.1 | convolution fusion | flops 14523826176 | bytes 37487616 | tf_op jit(solution)/shard_map/while/body/eval_jaxpr/dot_general | solution.py:51
  190.9 21.6 %bitcast_dynamic-update-slice_fusion.2 = bf16[4,6912,2048]{2,1,0:T(8,128)(2,1)} fusion(bf16[4,6912,2048]{2,1,0:T(8,128)(2,1)} %get-tuple-element.73, s32[]{:T(128)} %get-tuple-element.72, bf16[2048,512]{1,0:T(8,128)(2,1)S(1)} %get-tuple-element.80, bf16[4,6912,512]{2,1,0:T(8,128)(2,1)} %get-tuple-element.79), kind=kOutput, calls=%fused_computation.2.clone.1 | convolution fusion | flops 14523826176 | bytes 37487616 | tf_op jit(solution)/shard_map/while/body/eval_jaxpr/dot_general | solution.py:51
  212.5 42.6 %fusion.3 = bf16[4,8,27648]{2,1,0:T(8,128)(2,1)S(1)} fusion(bf16[27648,2048]{1,0:T(8,128)(2,1)} %bitcast.3, bf16[2048,32]{0,1:T(8,128)(2,1)S(1)} %copy-done), kind=kOutput, calls=%fused_computation.7 | convolution fusion | flops 3624763392 | bytes 115146752 | tf_op jit(solution)/shard_map/dot_general | solution.py:59
  255.1 23.7 %all_to_all.65 = bf16[4,8,27648]{2,1,0:T(8,128)(2,1)S(1)} all-to-all(bf16[4,8,27648]{2,1,0:T(8,128)(2,1)S(1)} %fusion.3), channel_id=1, replica_groups=mesh['grid'=8,'vec'=4] {'vec'}, dimensions={0} | all-to-all | bytes 3538944 | tf_op jit(solution)/shard_map/all_to_all | solution.py:62
  278.9 2.6 copy.77
  281.5 4.0 reshape.103
  292.5 5.2 copy.82
  297.7 4.6 all-to-all-start.1
  302.9 104.7 %all-to-all-done.1 = bf16[2,8,12,96,96]{4,1,2,0,3:T(8,128)(2,1)} async-done(((bf16[2,8,12,96,96]{4,1,2,0,3:T(8,128)(2,1)}), bf16[2,8,12,96,96]{4,1,2,0,3:T(8,128)(2,1)}, u32[]{:S(2)}, u32[]{:S(2)}) %all-to-all-start.1) | async-done | bytes 3538976 | tf_op jit(solution)/shard_map/all_to_all | solution.py:75
  407.6 3.6 copy.83
  412.2 2.0 fusion.32
  414.4 2.0 fusion.28
  416.4 2.4 fusion.6
  419.8 2.4 fusion.7
  426.5 3.0 copy.98
  429.5 107.7 %all_to_all.66 = bf16[2,8,96,12,96]{4,1,3,0,2:T(8,128)(2,1)S(1)} all-to-all(bf16[2,8,96,12,96]{4,1,3,0,2:T(8,128)(2,1)S(1)} %copy.98), channel_id=1, replica_groups=mesh['grid'=8,'vec'=4] {'grid'}, dimensions={2} | all-to-all | bytes 7077888 | tf_op jit(solution)/shard_map/all_to_all | solution.py:84
  539.1 3.2 fusion.26
  543.9 3.1 fusion.20
  547.1 7.1 %fusion.11 = f32[8,12,96,96]{3,2,1,0:T(8,128)} fusion(f32[96,8,12,96]{3,0,2,1:T(8,128)} %fusion.26, bf16[8,12,96,96]{3,0,2,1:T(8,128)(2,1)} %bitcast.130), kind=kOutput, calls=%fused_computation.27 | convolution fusion | flops 341692416 | bytes 8847360 | tf_op jit(solution)/shard_map/vxyz,zk->vxyk/dot_general | solution.py:33
  554.2 5.9 multiply_convert_fusion.1
  560.1 5.0 all_to_all.57
  565.6 24.6 %all_to_all.67 = bf16[8,4,27648]{2,0,1:T(8,128)(2,1)S(1)} all-to-all(bf16[8,4,27648]{2,0,1:T(8,128)(2,1)S(1)} %copy.110), channel_id=1, replica_groups=mesh['grid'=8,'vec'=4] {'vec'}, dimensions={1} | all-to-all | bytes 3538944 | tf_op jit(solution)/shard_map/all_to_all | solution.py:93
  590.2 38.7 %convolution_multiply_fusion = f32[2048,32]{0,1:T(8,128)} fusion(bf16[27648,2048]{1,0:T(8,128)(2,1)} %bitcast.3, bf16[8,4,27648]{2,0,1:T(8,128)(2,1)S(1)} %all_to_all.67), kind=kOutput, calls=%fused_computation.32 | convolution fusion | flops 3623944192 | bytes 115277824 | tf_op jit(solution)/shard_map/dot_general | solution.py:95
  629.0 28.7 %reduce-scatter.5.cloned.1.call-done = f32[256,32]{0,1:T(8,128)} async-done(((f32[2048,32]{0,1:T(8,128)}), f32[256,32]{0,1:T(8,128)}) %reduce-scatter.5.cloned.1.call-update) | async-done | bytes 32784 | tf_op jit(solution)/shard_map/reduce_scatter | solution.py:98
  657.7 1.5 copy.145
  659.2 23.5 %reduce-scatter.7.cloned.1.call-done = f32[64,32]{1,0:T(8,128)} async-done(((f32[256,32]{1,0:T(8,128)}), f32[64,32]{1,0:T(8,128)}) %reduce-scatter.7.cloned.1.call-update) | async-done | bytes 8208
  (38 shorter events, 21.1 us)
Async XLA Ops:
  6.5 206.0 %copy-start = (bf16[2048,32]{0,1:T(8,128)(2,1)S(1)}, bf16[2048,32]{0,1:T(8,128)(2,1)}, u32[]{:S(2)}) copy-start(bf16[2048,32]{0,1:T(8,128)(2,1)} %param.6) | copy-start | bytes 393220
  297.7 109.8 %all-to-all-start.1 = ((bf16[2,8,12,96,96]{4,1,2,0,3:T(8,128)(2,1)}), bf16[2,8,12,96,96]{4,1,2,0,3:T(8,128)(2,1)}, u32[]{:S(2)}, u32[]{:S(2)}) async-start(bf16[2,8,12,96,96]{4,1,2,0,3:T(8,128)(2,1)} %copy.82), calls=%async_computation.1 | async-start | bytes 9437184 | tf_op jit(solution)/shard_map/all_to_all | solution.py:75
  302.3 355.4 %reduce-scatter.5.cloned.1.call-start = ((), (), s32[]{:S(2)}) async-start(), calls=%async_computation.6 | async-start | bytes 294912 | tf_op jit(solution)/shard_map/reduce_scatter | solution.py:98
  542.5 1.4 copy-start.2
  590.2 94.0 %copy-start.1 = (bf16[2048,32]{0,1:T(8,128)(2,1)S(1)}, bf16[2048,32]{0,1:T(8,128)(2,1)}, u32[]{:S(2)}) copy-start(bf16[2048,32]{0,1:T(8,128)(2,1)} %param.6) | copy-start | bytes 393220
  628.9 53.8 %reduce-scatter.7.cloned.1.call-start = ((), (), s32[]{:S(2)}) async-start(), calls=%async_computation.7 | async-start | bytes 163840
Sparse Core Ops, SparseCore 0:
  629.1 28.6 reduce-scatter.4
  660.5 22.2 reduce-scatter.6
where the time goes:
time: 697 us; the launch traced here: 691 us
  blocking collectives  251 us (36%)
  matrix products  206 us (30%)
  waiting for transfers between devices  157 us (23%)
  local copies, waits for them, and re-layouts  51.9 us (7%)
  between operations  14.1 us (2%)
  other arithmetic  7.31 us (1%)
    all_to_all x1, blocking collectives, shards(): lax.all_to_all(jnp.stack([i_re, i_im]), 'grid', split_axis=2, concat_axis...  108 us
    all_to_all x1, waiting for transfers between devices, shards(): lax.all_to_all(stacked, 'grid', split_axis=3, concat_axis=2, tiled=True)  105 us
    psum x1, blocking collectives, shards(): summed_rows = lax.psum(picked, ('grid', 'vec'))  94.7 us
    dot_general x4, matrix products, pair_block(): lax.dot_general(block, point_rows, (((1,), (1,)), ((), ())), preferred_el...  86.1 us
    dot_general x1, matrix products, shards(): lax.dot_general(inverse_panel, pair, (((0,), (1,)), ((), ())), preferred_...  42.6 us
    dot_general x1, matrix products, shards(): lax.dot_general(pair, pot_rows, (((0,), (1,)), ((), ())), preferred_eleme...  38.7 us
    dot_general x18, matrix products, mult(): return jnp.einsum(form, data, table, preferred_element_type=jnp.float32)  38.2 us
    reduce_scatter x1, waiting for transfers between devices, shards(): lax.psum_scatter(term * jnp.float32(scale), 'grid', scatter_dimension=0,...  28.7 us
  transfers between devices with their start and end apart: 3, of which 3 were waited for; matrix products, arithmetic and copies ran while one was open for 0% of the time, Pallas kernels for 0%

commit v1 on v0

--- a/solution.py
+++ b/solution.py
@@ -44,7 +44,9 @@
     inside = (local_pos >= 0) & (local_pos < row_count)
     picked = jnp.take(orbitals, jnp.clip(local_pos, 0, row_count - 1), axis=0)
     picked = jnp.where(inside[:, None], picked, jnp.zeros_like(picked)).astype(jnp.float32)
-    summed_rows = lax.psum(picked, ("grid", "vec"))
+    summed_rows = picked
+    for axis in ("vec", "grid"):
+        summed_rows = lax.psum(summed_rows, axis)
     point_rows = summed_rows.astype(bf)
 
     def pair_block(block):

time: 697 us -> 800 us (1.15)
  waiting for transfers between devices: 157 us -> 255 us
  starting transfers between devices: 4.87 us -> 14.7 us
  blocking collectives: 251 us -> 243 us
    psum x0 -> x1, waiting for transfers between devices: none -> 106 us  [shards(): summed_rows = lax.psum(summed_rows, axis)]
    reduce_scatter x1, starting transfers between devices: 0.21 us -> 8.78 us  [shards(): lax.psum_scatter(term * jnp.float32(scale), 'grid', scatter_dimension=0,...]
    all_to_all x1, waiting for transfers between devices: 105 us -> 96.2 us  [shards(): lax.all_to_all(stacked, 'grid', split_axis=3, concat_axis=2, tiled=True)]
    unnamed x3 -> x4, waiting for transfers between devices: 23.6 us -> 23.7 us
  transfers between devices with their start and end apart: 3 -> 4, of which waited for: 3 -> 4; matrix products, arithmetic and copies ran while one was open for 0% -> 0% of each run, Pallas kernels for 0% -> 0%
where the time goes in v1:
time: 800 us; the launch traced here: 791 us
  waiting for transfers between devices  255 us (32%)
  blocking collectives  243 us (30%)
  matrix products  206 us (26%)
  local copies, waits for them, and re-layouts  51.5 us (6%)
  starting transfers between devices  14.7 us (2%)
  between operations  13.8 us (2%)
    all_to_all x1, blocking collectives, shards(): lax.all_to_all(jnp.stack([i_re, i_im]), 'grid', split_axis=2, concat_axis...  108 us
    psum x1, waiting for transfers between devices, shards(): summed_rows = lax.psum(summed_rows, axis)  106 us
    all_to_all x1, waiting for transfers between devices, shards(): lax.all_to_all(stacked, 'grid', split_axis=3, concat_axis=2, tiled=True)  96.2 us
    psum x1, blocking collectives, shards(): summed_rows = lax.psum(summed_rows, axis)  88.9 us
    dot_general x4, matrix products, pair_block(): lax.dot_general(block, point_rows, (((1,), (1,)), ((), ())), preferred_el...  86.1 us
    dot_general x1, matrix products, shards(): lax.dot_general(inverse_panel, pair, (((0,), (1,)), ((), ())), preferred_...  42.6 us
    dot_general x1, matrix products, shards(): lax.dot_general(pair, pot_rows, (((0,), (1,)), ((), ())), preferred_eleme...  38.7 us
    dot_general x18, matrix products, mult(): return jnp.einsum(form, data, table, preferred_element_type=jnp.float32)  38.2 us
  transfers between devices with their start and end apart: 4, of which 4 were waited for; matrix products, arithmetic and copies ran while one was open for 0% of the time, Pallas kernels for 0%

profile of v1, /device:TPU:0, one launch (start us, length us, event | category | flops | bytes accessed | tf_op | source)
XLA Modules:
  0.0 790.9 jit_solution(69470794796828960)
XLA Ops:
  8.0 20.3 %gather_fusion = bf16[2048,512]{1,0:T(8,128)(2,1)S(1)} fusion(bf16[27648,512]{1,0:T(8,128)(2,1)} %param.5, s32[2048]{0:T(1024)S(1)} %fusion.73), kind=kCustom, calls=%fused_computation | custom fusion | bytes 4202496 | tf_op jit(solution)/shard_map/jit(_take)/gather | solution.py:45
  28.3 3.5 select_convert_fusion
  31.8 106.5 %all-reduce.3.cloned.1.call-done = f32[2048,512]{1,0:T(8,128)} async-done(((f32[2048,512]{1,0:T(8,128)}), f32[2048,512]{1,0:T(8,128)}) %all-reduce.3.cloned.1.call-update) | async-done | bytes 4194320 | tf_op jit(solution)/shard_map/psum | solution.py:49
  138.2 88.9 %all-reduce.4 = bf16[2048,512]{1,0:T(8,128)(2,1)S(1)} all-reduce(f32[2048,512]{1,0:T(8,128)} %all-reduce.3.cloned.1.call-done), channel_id=1, replica_groups=mesh['grid'=8,'vec'=4] {'grid'}, use_global_device_ids=true, to_apply=%region_1.2 | all-reduce | flops 1048576 | bytes 6291456 | tf_op jit(solution)/shard_map/psum | solution.py:49
  227.1 86.1 %while.10 = (s32[]{:T(128)}, bf16[4,6912,2048]{2,1,0:T(8,128)(2,1)}, bf16[4,6912,512]{2,1,0:T(8,128)(2,1)}, bf16[2048,512]{1,0:T(8,128)(2,1)S(1)}, s32[]{:T(128)}) while((s32[]{:T(128)}, bf16[4,6912,2048]{2,1,0:T(8,128)(2,1)}, bf16[4,6912,512]{2,1,0:T(8,128)(2,1)}, bf16[2048,512]{1,0:T(8,128)(2,1)S(1)}, s32[]{:T(128)}) %tuple.30), condition=%wide.region_3.4_spmd, body=%wide.region_2.3_spmd.sunk | while | flops 14523826176 | bytes 37487676 | solution.py:58
  227.1 21.5 %bitcast_dynamic-update-slice_fusion.2 = bf16[4,6912,2048]{2,1,0:T(8,128)(2,1)} fusion(bf16[4,6912,2048]{2,1,0:T(8,128)(2,1)} %get-tuple-element.73, s32[]{:T(128)} %get-tuple-element.72, bf16[2048,512]{1,0:T(8,128)(2,1)S(1)} %get-tuple-element.80, bf16[4,6912,512]{2,1,0:T(8,128)(2,1)} %get-tuple-element.79), kind=kOutput, calls=%fused_computation.2.clone.1 | convolution fusion | flops 14523826176 | bytes 37487616 | tf_op jit(solution)/shard_map/while/body/eval_jaxpr/dot_general | solution.py:53
  248.6 21.4 %bitcast_dynamic-update-slice_fusion.2 = bf16[4,6912,2048]{2,1,0:T(8,128)(2,1)} fusion(bf16[4,6912,2048]{2,1,0:T(8,128)(2,1)} %get-tuple-element.73, s32[]{:T(128)} %get-tuple-element.72, bf16[2048,512]{1,0:T(8,128)(2,1)S(1)} %get-tuple-element.80, bf16[4,6912,512]{2,1,0:T(8,128)(2,1)} %get-tuple-element.79), kind=kOutput, calls=%fused_computation.2.clone.1 | convolution fusion | flops 14523826176 | bytes 37487616 | tf_op jit(solution)/shard_map/while/body/eval_jaxpr/dot_general | solution.py:53
  270.1 21.5 %bitcast_dynamic-update-slice_fusion.2 = bf16[4,6912,2048]{2,1,0:T(8,128)(2,1)} fusion(bf16[4,6912,2048]{2,1,0:T(8,128)(2,1)} %get-tuple-element.73, s32[]{:T(128)} %get-tuple-element.72, bf16[2048,512]{1,0:T(8,128)(2,1)S(1)} %get-tuple-element.80, bf16[4,6912,512]{2,1,0:T(8,128)(2,1)} %get-tuple-element.79), kind=kOutput, calls=%fused_computation.2.clone.1 | convolution fusion | flops 14523826176 | bytes 37487616 | tf_op jit(solution)/shard_map/while/body/eval_jaxpr/dot_general | solution.py:53
  291.6 21.6 %bitcast_dynamic-update-slice_fusion.2 = bf16[4,6912,2048]{2,1,0:T(8,128)(2,1)} fusion(bf16[4,6912,2048]{2,1,0:T(8,128)(2,1)} %get-tuple-element.73, s32[]{:T(128)} %get-tuple-element.72, bf16[2048,512]{1,0:T(8,128)(2,1)S(1)} %get-tuple-element.80, bf16[4,6912,512]{2,1,0:T(8,128)(2,1)} %get-tuple-element.79), kind=kOutput, calls=%fused_computation.2.clone.1 | convolution fusion | flops 14523826176 | bytes 37487616 | tf_op jit(solution)/shard_map/while/body/eval_jaxpr/dot_general | solution.py:53
  313.2 42.6 %fusion.3 = bf16[4,8,27648]{2,1,0:T(8,128)(2,1)S(1)} fusion(bf16[27648,2048]{1,0:T(8,128)(2,1)} %bitcast.3, bf16[2048,32]{0,1:T(8,128)(2,1)S(1)} %copy-done), kind=kOutput, calls=%fused_computation.7 | convolution fusion | flops 3624763392 | bytes 115146752 | tf_op jit(solution)/shard_map/dot_general | solution.py:61
  355.9 21.6 %all_to_all.65 = bf16[4,8,27648]{2,1,0:T(8,128)(2,1)S(1)} all-to-all(bf16[4,8,27648]{2,1,0:T(8,128)(2,1)S(1)} %fusion.3), channel_id=1, replica_groups=mesh['grid'=8,'vec'=4] {'vec'}, dimensions={0} | all-to-all | bytes 3538944 | tf_op jit(solution)/shard_map/all_to_all | solution.py:64
  377.5 2.6 copy.77
  380.1 3.6 reshape.103
  390.7 5.2 copy.82
  395.9 5.9 all-to-all-start.1
  401.8 8.8 %reduce-scatter.5.cloned.1.call-start = ((), (), s32[]{:S(2)}) async-start(), calls=%async_computation.7 | async-start | bytes 294912 | tf_op jit(solution)/shard_map/reduce_scatter | solution.py:100
  410.9 96.2 %all-to-all-done.1 = bf16[2,8,12,96,96]{4,1,2,0,3:T(8,128)(2,1)} async-done(((bf16[2,8,12,96,96]{4,1,2,0,3:T(8,128)(2,1)}), bf16[2,8,12,96,96]{4,1,2,0,3:T(8,128)(2,1)}, u32[]{:S(2)}, u32[]{:S(2)}) %all-to-all-start.1) | async-done | bytes 3538976 | tf_op jit(solution)/shard_map/all_to_all | solution.py:77
  507.1 3.6 copy.83
  514.0 2.0 fusion.28
  515.9 2.4 fusion.6
  519.3 2.4 fusion.7
  526.0 3.0 copy.98
  529.1 107.7 %all_to_all.66 = bf16[2,8,96,12,96]{4,1,3,0,2:T(8,128)(2,1)S(1)} all-to-all(bf16[2,8,96,12,96]{4,1,3,0,2:T(8,128)(2,1)S(1)} %copy.98), channel_id=1, replica_groups=mesh['grid'=8,'vec'=4] {'grid'}, dimensions={2} | all-to-all | bytes 7077888 | tf_op jit(solution)/shard_map/all_to_all | solution.py:86
  638.7 3.2 fusion.26
  643.5 3.1 fusion.20
  646.6 7.1 fusion.11
  653.7 5.9 multiply_convert_fusion.1
  659.6 5.0 all_to_all.57
  665.1 24.6 %all_to_all.67 = bf16[8,4,27648]{2,0,1:T(8,128)(2,1)S(1)} all-to-all(bf16[8,4,27648]{2,0,1:T(8,128)(2,1)S(1)} %copy.110), channel_id=1, replica_groups=mesh['grid'=8,'vec'=4] {'vec'}, dimensions={1} | all-to-all | bytes 3538944 | tf_op jit(solution)/shard_map/all_to_all | solution.py:95
  689.8 38.7 %convolution_multiply_fusion = f32[2048,32]{0,1:T(8,128)} fusion(bf16[27648,2048]{1,0:T(8,128)(2,1)} %bitcast.3, bf16[8,4,27648]{2,0,1:T(8,128)(2,1)S(1)} %all_to_all.67), kind=kOutput, calls=%fused_computation.32 | convolution fusion | flops 3623944192 | bytes 115277824 | tf_op jit(solution)/shard_map/dot_general | solution.py:97
  728.5 28.8 %reduce-scatter.5.cloned.1.call-done = f32[256,32]{0,1:T(8,128)} async-done(((f32[2048,32]{0,1:T(8,128)}), f32[256,32]{0,1:T(8,128)}) %reduce-scatter.5.cloned.1.call-update) | async-done | bytes 32784 | tf_op jit(solution)/shard_map/reduce_scatter | solution.py:100
  758.8 23.6 %reduce-scatter.7.cloned.1.call-done = f32[64,32]{1,0:T(8,128)} async-done(((f32[256,32]{1,0:T(8,128)}), f32[64,32]{1,0:T(8,128)}) %reduce-scatter.7.cloned.1.call-update) | async-done | bytes 8208
  (41 shorter events, 24.3 us)
Async XLA Ops:
  6.5 306.7 %copy-start = (bf16[2048,32]{0,1:T(8,128)(2,1)S(1)}, bf16[2048,32]{0,1:T(8,128)(2,1)}, u32[]{:S(2)}) copy-start(bf16[2048,32]{0,1:T(8,128)(2,1)} %param.6) | copy-start | bytes 393220
  6.5 131.7 %all-reduce.3.cloned.1.call-start = ((), (), s32[]{:S(2)}) async-start(), calls=%async_computation.6 | async-start | bytes 8388608 | tf_op jit(solution)/shard_map/psum | solution.py:49
  395.9 111.2 %all-to-all-start.1 = ((bf16[2,8,12,96,96]{4,1,2,0,3:T(8,128)(2,1)}), bf16[2,8,12,96,96]{4,1,2,0,3:T(8,128)(2,1)}, u32[]{:S(2)}, u32[]{:S(2)}) async-start(bf16[2,8,12,96,96]{4,1,2,0,3:T(8,128)(2,1)} %copy.82), calls=%async_computation.1 | async-start | bytes 9437184 | tf_op jit(solution)/shard_map/all_to_all | solution.py:77
  401.8 355.5 %reduce-scatter.5.cloned.1.call-start = ((), (), s32[]{:S(2)}) async-start(), calls=%async_computation.7 | async-start | bytes 294912 | tf_op jit(solution)/shard_map/reduce_scatter | solution.py:100
  642.1 1.4 copy-start.2
  689.8 94.1 %copy-start.1 = (bf16[2048,32]{0,1:T(8,128)(2,1)S(1)}, bf16[2048,32]{0,1:T(8,128)(2,1)}, u32[]{:S(2)}) copy-start(bf16[2048,32]{0,1:T(8,128)(2,1)} %param.6) | copy-start | bytes 393220
  728.5 54.0 %reduce-scatter.7.cloned.1.call-start = ((), (), s32[]{:S(2)}) async-start(), calls=%async_computation.8 | async-start | bytes 163840
Sparse Core Ops, SparseCore 0:
  31.9 106.3 all-reduce.2
  728.6 28.6 reduce-scatter.4
  760.0 22.3 reduce-scatter.6
